TPU v7x, 32 devices: a whole 2x2x4 slice. The times are simulated.
32 devices in a mesh: blk: 8 (over y, x, core), grp: 4 (over z).
Axes of the slice: x: 2, y: 2, z: 4, core: 2. Of those that a mesh axis runs over, the one named last changes fastest.
Arguments:
- node_feats: bfloat16 [8192, 512], P(('blk', 'grp')), may hold values from -6 to 6
- w_local: bfloat16 [512, 512], replicated, may hold values from -0.25 to 0.25
- w_gate: bfloat16 [512, 512], replicated, may hold values from -0.25 to 0.25
- w_query: bfloat16 [512, 512], replicated, may hold values from -0.25 to 0.25
- w_key: bfloat16 [512, 512], replicated, may hold values from -0.25 to 0.25
- w_value: bfloat16 [512, 512], replicated, may hold values from -0.25 to 0.25
- norm_gain: float32 [512], replicated, may hold values from 0.1 to 1.9
- tile_weights: int32 [8, 8, 4, 8, 128, 128], P('blk', None, 'grp'), may hold values from 0 to 2
- tile_slots: int32 [8, 8, 4, 8], P('blk', None, 'grp'), may hold values from 0 to 15, as said below
- tile_counts: int32 [8, 8, 4], P('blk', None, 'grp'), may hold values from 1 to 8, as said below
Outputs:
- layer_out: bfloat16 [8192, 512], P(('blk', 'grp'))
Inputs may be any that keep to these rules, and one draw needn't show every extreme that they name: `tile_counts`: some block pair has all 8 slots live in every draw. `tile_slots`: the 8 slots of one block pair name different tile positions.
All inputs are finite; a program needn't handle non-finite values.
Results may differ from a plain program's by a relative error of at most 0.0085.
Values may be sent and summed in bfloat16 or wider, within the bound.
No kernel may reach another device: no remote copies, remote signals or barrier semaphores. Data moves between devices by JAX's collectives and lax.ppermute only.
A program may use at most 128 MiB of HBM per device.

v0:
```python
import jax
import jax.numpy as jnp
from jax import lax
from jax.sharding import PartitionSpec as P

HEADS = 8
HOPS = 2


norm_eps = 1e-05


def from_behind(block, axis, distance):
    devices = range(lax.axis_size(axis))
    route = [((i - distance) % len(devices), i) for i in devices]
    return lax.ppermute(block, axis, route)


def send_along(along_piece):
    return from_behind(along_piece, "blk", 1)


def local(
    node_feats,
    w_local,
    w_gate,
    w_query,
    w_key,
    w_value,
    norm_gain,
    tile_weights,
    tile_slots,
    tile_counts,
):
    row_count, feat_width = node_feats.shape
    tile_size = tile_weights.shape[-1]
    slot_most = tile_weights.shape[3]
    blocks = lax.axis_size("blk")
    groups = lax.axis_size("grp")
    col_tiles = row_count // tile_size
    row_tiles = groups * col_tiles
    my_block = lax.axis_index("blk")
    counts = tile_counts[0, :, 0]
    slot_ids = tile_slots[0, :, 0]
    weights = tile_weights[0, :, 0]
    live_slots = jnp.arange(slot_most, dtype=jnp.int32)[None, :] < counts[:, None]
    masked = jnp.where(live_slots[:, :, None, None], weights, 0)
    tiles_bf = masked.astype(jnp.bfloat16)
    row_index = slot_ids // col_tiles
    col_index = slot_ids % col_tiles
    rows_pick = (row_index[..., None] == jnp.arange(row_tiles, dtype=jnp.int32)).astype(jnp.float32)
    row_weight = jnp.sum(masked, axis=-1).astype(jnp.float32)
    degree_part = jnp.einsum(
        "jtr,jti->ri", rows_pick, row_weight, precision=lax.Precision.HIGHEST
    ).reshape(row_tiles * tile_size)

    def accumulate(partial_value, block_piece, source):
        source = jnp.mod(source, blocks)
        tile_block = lax.dynamic_index_in_dim(tiles_bf, source, 0, keepdims=False)
        rows_here = lax.dynamic_index_in_dim(row_index, source, 0, keepdims=False)
        cols_here = lax.dynamic_index_in_dim(col_index, source, 0, keepdims=False)
        stacked = block_piece.reshape(col_tiles, tile_size, feat_width)
        chosen = jnp.take(stacked, cols_here, axis=0)
        product = jnp.einsum("til,tld->tid", tile_block, chosen, preferred_element_type=jnp.float32)
        for slot in range(slot_most):
            target = rows_here[slot]
            current = lax.dynamic_index_in_dim(partial_value, target, 0, keepdims=False)
            partial_value = lax.dynamic_update_index_in_dim(
                partial_value, current + product[slot], target, 0
            )
        return partial_value

    def one_hop(feats):
        empty = jnp.zeros((row_tiles, tile_size, feat_width), jnp.float32)

        def turn(step_index, loop_state):
            along_piece, partial_value = loop_state
            partial_value = accumulate(partial_value, along_piece, my_block - step_index)
            along_piece = send_along(along_piece)
            return (along_piece, partial_value)

        along_piece, partial_value = lax.fori_loop(0, blocks - 1, turn, (feats, empty))
        partial_value = accumulate(partial_value, along_piece, my_block - (blocks - 1))
        return partial_value.reshape(row_tiles * tile_size, feat_width)

    feats = jnp.dot(node_feats, w_local, preferred_element_type=jnp.float32).astype(jnp.bfloat16)
    scale = None
    for hop_index in range(HOPS):
        flat = one_hop(feats)
        if hop_index == 0:
            summed, degree_rows = (
                lax.psum_scatter(flat, "grp", scatter_dimension=0, tiled=True),
                lax.psum_scatter(degree_part, "grp", scatter_dimension=0, tiled=True),
            )
            scale = lax.rsqrt(degree_rows + 1.0)
        else:
            summed = lax.psum_scatter(flat, "grp", scatter_dimension=0, tiled=True)
        feats = ((summed + feats.astype(jnp.float32)) * scale[:, None]).astype(jnp.bfloat16)
    head_size = feat_width // HEADS
    queries = jax.nn.sigmoid(
        jnp.dot(node_feats, w_query, preferred_element_type=jnp.float32)
    ).astype(jnp.bfloat16)
    keys_here = jax.nn.sigmoid(
        jnp.dot(node_feats, w_key, preferred_element_type=jnp.float32)
    ).astype(jnp.bfloat16)
    values_here = jnp.dot(node_feats, w_value, preferred_element_type=jnp.float32).astype(
        jnp.bfloat16
    )
    queries = queries.reshape(row_count, HEADS, head_size)
    keys_here = keys_here.reshape(row_count, HEADS, head_size)
    values_here = values_here.reshape(row_count, HEADS, head_size)
    local_sum = jnp.einsum(
        "nhd,nhe->hde", keys_here, values_here, preferred_element_type=jnp.float32
    )
    local_flat = local_sum.reshape(HEADS, head_size * head_size)
    summary = lax.psum(local_flat, ("blk", "grp"))
    summary_b = summary.astype(jnp.bfloat16).reshape(HEADS, head_size, head_size)
    attended = jnp.einsum(
        "nhd,hde->nhe", queries, summary_b, preferred_element_type=jnp.float32
    ).reshape(row_count, feat_width)
    mean_val = jnp.mean(attended, axis=1, keepdims=True)
    centered = attended - mean_val
    var_val = jnp.mean(centered * centered, axis=1, keepdims=True)
    glob = centered * lax.rsqrt(var_val + norm_eps) * norm_gain[None, :]
    gate = jnp.dot(node_feats, w_gate, preferred_element_type=jnp.float32)
    total = node_feats.astype(jnp.float32) + feats.astype(jnp.float32) * gate + glob
    return total.astype(jnp.bfloat16)


def solution(mesh):
    in_specs = (
        P(("blk", "grp"), None),
        P(),
        P(),
        P(),
        P(),
        P(),
        P(),
        P("blk", None, "grp", None, None, None),
        P("blk", None, "grp", None),
        P("blk", None, "grp"),
    )
    out_specs = P(("blk", "grp"), None)
    return jax.shard_map(local, mesh=mesh, in_specs=in_specs, out_specs=out_specs, check_vma=False)
```

profile of v0, /device:TPU:0, one launch (start us, length us, event | category | flops | bytes accessed | tf_op | source)
XLA Modules:
  0.0 626.4 jit_solution(9930929994625450928)
XLA Ops:
  20.1 4.2 fusion.34
  25.9 237.5 %while.34 = (s32[]{:T(128)}, bf16[256,512]{1,0:T(8,128)(2,1)S(1)}, f32[8,128,512]{2,1,0:T(8,128)}, s32[]{:T(128)}, s32[8,8]{1,0:T(8,128)S(1)}, /*index=5*/bf16[8...) while((s32[]{:T(128)}, bf16[256,512]{1,0:T(8,128)(2,1)S(1)}, ...), condition=%wide.region_1.3_spmd, body=%wide.region_0.2_spmd.sunk | while | flops 135267392 | bytes 13374332 | solution.py:82
  38.9 1.8 fusion.133
  59.5 2.6 collective-permute-start
  74.5 1.8 fusion.133
  107.5 1.8 fusion.133
  142.2 1.8 fusion.133
  175.3 1.8 fusion.133
  209.8 1.8 fusion.133
  242.9 1.8 fusion.133
  265.0 3.3 fusion.49
  284.4 12.3 %all-reduce = f32[1024]{0:T(1024)S(1)} all-reduce(f32[1024]{0:T(1024)S(1)} %convolution_bitcast_fusion), channel_id=3, replica_groups=mesh['blk'=8,'grp'=4] {'grp'}, use_global_device_ids=true, to_apply=%region_4.6.clone | all-reduce | flops 1024 | bytes 8192
  296.8 31.4 %reduce-scatter.3.cloned.1.call-done = f32[256,512]{1,0:T(8,128)} async-done(((f32[1024,512]{1,0:T(8,128)}), f32[256,512]{1,0:T(8,128)}) %reduce-scatter.3.cloned.1.call-update) | async-done | bytes 524304 | tf_op jit(solution)/shard_map/reduce_scatter | solution.py:92
  330.9 234.5 %while.35 = (s32[]{:T(128)}, bf16[256,512]{1,0:T(8,128)(2,1)S(1)}, f32[8,128,512]{2,1,0:T(8,128)}, s32[]{:T(128)}, s32[8,8]{1,0:T(8,128)S(1)}, /*index=5*/bf16[8...) while((s32[]{:T(128)}, bf16[256,512]{1,0:T(8,128)(2,1)S(1)}, ...), condition=%wide.region_6.8_spmd, body=%wide.region_5.7_spmd.sunk | while | flops 135267392 | bytes 13374332 | solution.py:82
  343.3 1.8 fusion.145
  349.2 1.7 fusion.148
  377.6 1.8 fusion.145
  383.5 1.7 fusion.148
  410.5 1.8 fusion.145
  420.9 1.7 fusion.150
  444.9 1.8 fusion.145
  463.6 1.7 fusion.153
  477.8 1.8 fusion.145
  490.6 1.7 fusion.151
  492.9 1.7 fusion.152
  512.1 1.8 fusion.145
  518.0 1.7 fusion.148
  544.9 1.8 fusion.145
  546.8 1.7 fusion.146
  567.0 1.9 fusion.47
  573.3 42.5 %all-reduce.2 = bf16[8,4096]{1,0:T(8,128)(2,1)S(1)} all-reduce(f32[8,4096]{1,0:T(8,128)S(1)} %reshape.184), channel_id=1, replica_groups=mesh['blk'=8,'grp'=4] {'blk','grp'}, use_global_device_ids=true, to_apply=%region_8.10 | all-reduce | flops 32768 | bytes 196608 | tf_op jit(solution)/shard_map/psum | solution.py:116
  617.5 2.1 fusion.44
  (294 shorter events, 244.9 us)
Async XLA Ops:
  6.5 12.3 %copy-start = (bf16[512,512]{1,0:T(8,128)(2,1)S(1)}, bf16[512,512]{1,0:T(8,128)(2,1)}, u32[]{:S(2)}) copy-start(bf16[512,512]{1,0:T(8,128)(2,1)} %param.17) | copy-start | bytes 1572868
  6.5 321.6 %reduce-scatter.3.cloned.1.call-start = ((), (), s32[]{:S(2)}) async-start(), calls=%async_computation.2 | async-start | bytes 2621440 | tf_op jit(solution)/shard_map/reduce_scatter | solution.py:92
  20.1 4.3 copy-start.5
  24.3 1.6 copy-start.7
  25.9 33.5 %collective-permute-start = (bf16[256,512]{1,0:T(8,128)(2,1)S(1)}, bf16[256,512]{1,0:T(8,128)(2,1)S(1)}, u32[]{:S(2)}, u32[]{:S(2)}) collective-permute-start(bf16[256,512]{1,0:T(8,128)(2,1)S(1)} %copy.47), channel_id=1, source_target_pairs={{28,0},{0,4},{4,8},{8,12},{12,16},{16,20},{20,24},{24,28},{29,1},{... | collective-permute-start | bytes 786440 | tf_op jit(solution)/shard_map/while/body/eval_jaxpr/ppermute | solution.py:16
  59.5 35.5 %collective-permute-start = (bf16[256,512]{1,0:T(8,128)(2,1)S(1)}, bf16[256,512]{1,0:T(8,128)(2,1)S(1)}, u32[]{:S(2)}, u32[]{:S(2)}) collective-permute-start(bf16[256,512]{1,0:T(8,128)(2,1)S(1)} %copy.47), channel_id=1, source_target_pairs={{28,0},{0,4},{4,8},{8,12},{12,16},{16,20},{20,24},{24,28},{29,1},{... | collective-permute-start | bytes 786440 | tf_op jit(solution)/shard_map/while/body/eval_jaxpr/ppermute | solution.py:16
  95.0 33.0 %collective-permute-start = (bf16[256,512]{1,0:T(8,128)(2,1)S(1)}, bf16[256,512]{1,0:T(8,128)(2,1)S(1)}, u32[]{:S(2)}, u32[]{:S(2)}) collective-permute-start(bf16[256,512]{1,0:T(8,128)(2,1)S(1)} %copy.47), channel_id=1, source_target_pairs={{28,0},{0,4},{4,8},{8,12},{12,16},{16,20},{20,24},{24,28},{29,1},{... | collective-permute-start | bytes 786440 | tf_op jit(solution)/shard_map/while/body/eval_jaxpr/ppermute | solution.py:16
  128.1 34.6 %collective-permute-start = (bf16[256,512]{1,0:T(8,128)(2,1)S(1)}, bf16[256,512]{1,0:T(8,128)(2,1)S(1)}, u32[]{:S(2)}, u32[]{:S(2)}) collective-permute-start(bf16[256,512]{1,0:T(8,128)(2,1)S(1)} %copy.47), channel_id=1, source_target_pairs={{28,0},{0,4},{4,8},{8,12},{12,16},{16,20},{20,24},{24,28},{29,1},{... | collective-permute-start | bytes 786440 | tf_op jit(solution)/shard_map/while/body/eval_jaxpr/ppermute | solution.py:16
  162.7 33.1 %collective-permute-start = (bf16[256,512]{1,0:T(8,128)(2,1)S(1)}, bf16[256,512]{1,0:T(8,128)(2,1)S(1)}, u32[]{:S(2)}, u32[]{:S(2)}) collective-permute-start(bf16[256,512]{1,0:T(8,128)(2,1)S(1)} %copy.47), channel_id=1, source_target_pairs={{28,0},{0,4},{4,8},{8,12},{12,16},{16,20},{20,24},{24,28},{29,1},{... | collective-permute-start | bytes 786440 | tf_op jit(solution)/shard_map/while/body/eval_jaxpr/ppermute | solution.py:16
  195.8 34.5 %collective-permute-start = (bf16[256,512]{1,0:T(8,128)(2,1)S(1)}, bf16[256,512]{1,0:T(8,128)(2,1)S(1)}, u32[]{:S(2)}, u32[]{:S(2)}) collective-permute-start(bf16[256,512]{1,0:T(8,128)(2,1)S(1)} %copy.47), channel_id=1, source_target_pairs={{28,0},{0,4},{4,8},{8,12},{12,16},{16,20},{20,24},{24,28},{29,1},{... | collective-permute-start | bytes 786440 | tf_op jit(solution)/shard_map/while/body/eval_jaxpr/ppermute | solution.py:16
  230.3 33.1 %collective-permute-start = (bf16[256,512]{1,0:T(8,128)(2,1)S(1)}, bf16[256,512]{1,0:T(8,128)(2,1)S(1)}, u32[]{:S(2)}, u32[]{:S(2)}) collective-permute-start(bf16[256,512]{1,0:T(8,128)(2,1)S(1)} %copy.47), channel_id=1, source_target_pairs={{28,0},{0,4},{4,8},{8,12},{12,16},{16,20},{20,24},{24,28},{29,1},{... | collective-permute-start | bytes 786440 | tf_op jit(solution)/shard_map/while/body/eval_jaxpr/ppermute | solution.py:16
  265.0 4.5 copy-start.3
  277.1 5.7 copy-start.13
  277.2 51.0 %copy-start.6 = (bf16[256,512]{1,0:T(8,128)(2,1)S(1)}, bf16[256,512]{1,0:T(8,128)(2,1)}, u32[]{:S(2)}) copy-start(bf16[256,512]{1,0:T(8,128)(2,1)} %copy-done.5) | copy-start | bytes 786436
  281.5 1.3 copy-start.4
  282.8 334.4 %reduce-scatter.5.cloned.1.call-start = ((), (), s32[]{:S(2)}) async-start(), calls=%async_computation.3 | async-start | bytes 2621440 | tf_op jit(solution)/shard_map/reduce_scatter | solution.py:97
  330.9 32.8 %collective-permute-start.1 = (bf16[256,512]{1,0:T(8,128)(2,1)S(1)}, bf16[256,512]{1,0:T(8,128)(2,1)S(1)}, u32[]{:S(2)}, u32[]{:S(2)}) collective-permute-start(bf16[256,512]{1,0:T(8,128)(2,1)S(1)} %copy.64), channel_id=1, source_target_pairs={{28,0},{0,4},{4,8},{8,12},{12,16},{16,20},{20,24},{24,28},{29,1},{... | collective-permute-start | bytes 786440 | tf_op jit(solution)/shard_map/while/body/eval_jaxpr/ppermute | solution.py:16
  363.8 34.3 %collective-permute-start.1 = (bf16[256,512]{1,0:T(8,128)(2,1)S(1)}, bf16[256,512]{1,0:T(8,128)(2,1)S(1)}, u32[]{:S(2)}, u32[]{:S(2)}) collective-permute-start(bf16[256,512]{1,0:T(8,128)(2,1)S(1)} %copy.64), channel_id=1, source_target_pairs={{28,0},{0,4},{4,8},{8,12},{12,16},{16,20},{20,24},{24,28},{29,1},{... | collective-permute-start | bytes 786440 | tf_op jit(solution)/shard_map/while/body/eval_jaxpr/ppermute | solution.py:16
  398.1 32.9 %collective-permute-start.1 = (bf16[256,512]{1,0:T(8,128)(2,1)S(1)}, bf16[256,512]{1,0:T(8,128)(2,1)S(1)}, u32[]{:S(2)}, u32[]{:S(2)}) collective-permute-start(bf16[256,512]{1,0:T(8,128)(2,1)S(1)} %copy.64), channel_id=1, source_target_pairs={{28,0},{0,4},{4,8},{8,12},{12,16},{16,20},{20,24},{24,28},{29,1},{... | collective-permute-start | bytes 786440 | tf_op jit(solution)/shard_map/while/body/eval_jaxpr/ppermute | solution.py:16
  431.0 34.3 %collective-permute-start.1 = (bf16[256,512]{1,0:T(8,128)(2,1)S(1)}, bf16[256,512]{1,0:T(8,128)(2,1)S(1)}, u32[]{:S(2)}, u32[]{:S(2)}) collective-permute-start(bf16[256,512]{1,0:T(8,128)(2,1)S(1)} %copy.64), channel_id=1, source_target_pairs={{28,0},{0,4},{4,8},{8,12},{12,16},{16,20},{20,24},{24,28},{29,1},{... | collective-permute-start | bytes 786440 | tf_op jit(solution)/shard_map/while/body/eval_jaxpr/ppermute | solution.py:16
  465.3 33.0 %collective-permute-start.1 = (bf16[256,512]{1,0:T(8,128)(2,1)S(1)}, bf16[256,512]{1,0:T(8,128)(2,1)S(1)}, u32[]{:S(2)}, u32[]{:S(2)}) collective-permute-start(bf16[256,512]{1,0:T(8,128)(2,1)S(1)} %copy.64), channel_id=1, source_target_pairs={{28,0},{0,4},{4,8},{8,12},{12,16},{16,20},{20,24},{24,28},{29,1},{... | collective-permute-start | bytes 786440 | tf_op jit(solution)/shard_map/while/body/eval_jaxpr/ppermute | solution.py:16
  498.3 34.2 %collective-permute-start.1 = (bf16[256,512]{1,0:T(8,128)(2,1)S(1)}, bf16[256,512]{1,0:T(8,128)(2,1)S(1)}, u32[]{:S(2)}, u32[]{:S(2)}) collective-permute-start(bf16[256,512]{1,0:T(8,128)(2,1)S(1)} %copy.64), channel_id=1, source_target_pairs={{28,0},{0,4},{4,8},{8,12},{12,16},{16,20},{20,24},{24,28},{29,1},{... | collective-permute-start | bytes 786440 | tf_op jit(solution)/shard_map/while/body/eval_jaxpr/ppermute | solution.py:16
  532.6 32.9 %collective-permute-start.1 = (bf16[256,512]{1,0:T(8,128)(2,1)S(1)}, bf16[256,512]{1,0:T(8,128)(2,1)S(1)}, u32[]{:S(2)}, u32[]{:S(2)}) collective-permute-start(bf16[256,512]{1,0:T(8,128)(2,1)S(1)} %copy.64), channel_id=1, source_target_pairs={{28,0},{0,4},{4,8},{8,12},{12,16},{16,20},{20,24},{24,28},{29,1},{... | collective-permute-start | bytes 786440 | tf_op jit(solution)/shard_map/while/body/eval_jaxpr/ppermute | solution.py:16
  567.0 2.0 copy-start.1
  569.3 1.6 copy-start.8
  569.5 1.3 copy-start.2
  570.9 1.7 copy-start.9
  572.4 43.6 %copy-start.12 = (bf16[512,512]{1,0:T(8,128)(2,1)S(1)}, bf16[512,512]{1,0:T(8,128)(2,1)}, u32[]{:S(2)}) copy-start(bf16[512,512]{1,0:T(8,128)(2,1)} %param.19) | copy-start | bytes 1572868
  616.4 1.0 copy-start.10
  616.4 1.0 copy-start.11
Sparse Core Ops, SparseCore 0:
  282.9 45.1 reduce-scatter.2
  571.0 44.1 reduce-scatter.4
where the time goes:
time: 634 us; the launch traced here: 626 us
  loops' own time  212 us (33%)
  other arithmetic  206 us (32%)
  blocking collectives  54.8 us (9%)
  local copies, waits for them, and re-layouts  43.4 us (7%)
  matrix products  36.7 us (6%)
  waiting for transfers between devices  31.4 us (5%)
  between operations  29.6 us (5%)
  starting transfers between devices  12 us (2%)
    another operation x2, loops' own time, one_hop(): lax.fori_loop(0, blocks - 1, turn, (feats, empty))  212 us
    dynamic_update_slice x128, other arithmetic, accumulate(): lax.dynamic_update_index_in_dim(partial_value, current + product[slot], t...  199 us
    psum x1, blocking collectives, local(): summary = lax.psum(local_flat, ('blk', 'grp'))  42.5 us
    reduce_scatter x1, waiting for transfers between devices, local(): lax.psum_scatter(flat, 'grp', scatter_dimension=0, tiled=True)  31.4 us
    dot_general x16, matrix products, accumulate(): jnp.einsum('til,tld->tid', tile_block, chosen, preferred_element_type=jnp...  30.5 us
    gather x16, local copies, waits for them, and re-layouts, accumulate(): chosen = jnp.take(stacked, cols_here, axis=0)  25.3 us
  transfers between devices with their start and end apart: 16, of which 1 were waited for; matrix products, arithmetic and copies ran while one was open for 40% of the time, Pallas kernels for 0%

commit v1 on v0

v1 whole, which is shorter than its diff:
```python
import jax
import jax.numpy as jnp
from jax import lax
from jax.experimental import pallas as pl
from jax.experimental.pallas import tpu as pltpu
from jax.sharding import PartitionSpec as P

HEADS = 8
HOPS = 2
CHUNKS = 2


norm_eps = 1e-05


def swap(value, axis, mask):
    size = lax.axis_size(axis)
    return lax.ppermute(value, axis, [(i, i ^ mask) for i in range(size)])


def prepare(weights, slots, counts, my_block, row_tiles, col_tiles):
    blocks, slot_most, tile, _ = weights.shape
    rows, cols = row_tiles * tile, col_tiles * tile

    def kernel(me_ref, slots_ref, counts_ref, w_ref, a_ref, deg_ref, acc_ref):
        step = pl.program_id(0)
        source = me_ref[0] ^ step
        a_ref[...] = jnp.zeros_like(a_ref)

        @pl.when(step == 0)
        def _():
            acc_ref[...] = jnp.zeros_like(acc_ref)

        for slot in range(slot_most):

            @pl.when(slot < counts_ref[source])
            def _():
                place = slots_ref[source, slot]
                row = pl.multiple_of((place // col_tiles) * tile, tile)
                col = pl.multiple_of((place % col_tiles) * tile, tile)
                values = w_ref[0, slot].astype(jnp.float32)
                a_ref[pl.ds(row, tile), pl.ds(col, tile)] = values.astype(jnp.bfloat16)
                acc_ref[pl.ds(row, tile), :] += values

        @pl.when(step == blocks - 1)
        def _():
            ones = jnp.ones((8, tile), jnp.bfloat16)
            total = acc_ref[...].astype(jnp.bfloat16)
            deg_ref[...] = lax.dot_general(
                ones, total, (((1,), (1,)), ((), ())), preferred_element_type=jnp.float32
            )

    return pl.pallas_call(
        kernel,
        out_shape=(
            jax.ShapeDtypeStruct((rows, blocks * cols), jnp.bfloat16),
            jax.ShapeDtypeStruct((8, rows), jnp.float32),
        ),
        grid_spec=pltpu.PrefetchScalarGridSpec(
            num_scalar_prefetch=3,
            grid=(blocks,),
            in_specs=[
                pl.BlockSpec(
                    (1, slot_most, tile, tile), lambda s, me, sl, ct: (me[0] ^ s, 0, 0, 0)
                )
            ],
            out_specs=(
                pl.BlockSpec((rows, cols), lambda s, me, sl, ct: (0, s)),
                pl.BlockSpec((8, rows), lambda s, me, sl, ct: (0, 0)),
            ),
            scratch_shapes=[pltpu.VMEM((rows, tile), jnp.float32)],
        ),
        compiler_params=pltpu.CompilerParams(vmem_limit_bytes=16 << 20),
        cost_estimate=pl.CostEstimate(
            flops=rows * blocks * cols, bytes_accessed=weights.size * 4 + rows * blocks * cols * 2, transcendentals=0
        ),
        name="prepare",
    )(my_block, slots, counts, weights)


def local(
    node_feats,
    w_local,
    w_gate,
    w_query,
    w_key,
    w_value,
    norm_gain,
    tile_weights,
    tile_slots,
    tile_counts,
):
    row_count, feat_width = node_feats.shape
    tile_size = tile_weights.shape[-1]
    blocks = lax.axis_size("blk")
    groups = lax.axis_size("grp")
    col_tiles = row_count // tile_size
    row_tiles = groups * col_tiles
    my_block = lax.axis_index("blk")
    my_group = lax.axis_index("grp")
    width = feat_width // CHUNKS

    adjacency, degree_part = prepare(
        tile_weights[0, :, 0],
        tile_slots[0, :, 0],
        tile_counts[0, :, 0],
        my_block.astype(jnp.int32)[None],
        row_tiles,
        col_tiles,
    )
    degree = degree_part[0]
    step = 1
    while step < groups:
        degree = degree + swap(degree, "grp", step)
        step *= 2
    degree_rows = lax.dynamic_slice_in_dim(degree, my_group * row_count, row_count)
    scale = lax.rsqrt(degree_rows + 1.0)[:, None]

    def one_hop(feats):
        pieces = [feats] + [swap(feats, "blk", m) for m in range(2, blocks, 2)]
        mine = jnp.concatenate(pieces)
        other = swap(mine, "blk", 1)
        gathered = jnp.stack([mine.reshape(blocks // 2, row_count, -1), other.reshape(blocks // 2, row_count, -1)], axis=1)
        partial = jnp.dot(adjacency, gathered.reshape(blocks * row_count, -1), preferred_element_type=jnp.float32)
        partial = partial.reshape(groups, row_count, -1)

        def chunk(mask):
            return lax.dynamic_index_in_dim(partial, my_group ^ mask, 0, keepdims=False)

        total = chunk(0) + feats.astype(jnp.float32)
        for m in range(groups - 1, 0, -1):
            total = total + swap(chunk(m).astype(jnp.bfloat16), "grp", m).astype(jnp.float32)
        return (total * scale).astype(jnp.bfloat16)

    feats = jnp.dot(node_feats, w_local, preferred_element_type=jnp.float32).astype(jnp.bfloat16)
    columns = [feats[:, i * width : (i + 1) * width] for i in range(CHUNKS)]
    for hop_index in range(HOPS):
        columns = [one_hop(column) for column in columns]
    head_size = feat_width // HEADS
    queries = jax.nn.sigmoid(
        jnp.dot(node_feats, w_query, preferred_element_type=jnp.float32)
    ).astype(jnp.bfloat16)
    keys_here = jax.nn.sigmoid(
        jnp.dot(node_feats, w_key, preferred_element_type=jnp.float32)
    ).astype(jnp.bfloat16)
    values_here = jnp.dot(node_feats, w_value, preferred_element_type=jnp.float32).astype(
        jnp.bfloat16
    )
    queries = queries.reshape(row_count, HEADS, head_size)
    keys_here = keys_here.reshape(row_count, HEADS, head_size)
    values_here = values_here.reshape(row_count, HEADS, head_size)
    summary = jnp.einsum(
        "nhd,nhe->hde", keys_here, values_here, preferred_element_type=jnp.float32
    )
    summary = summary.reshape(-1, 128)
    for axis, size in (("blk", blocks), ("grp", groups)):
        step = 1
        while step < size:
            summary = summary + swap(summary, axis, step)
            step *= 2
    summary_b = summary.astype(jnp.bfloat16).reshape(HEADS, head_size, head_size)
    attended = jnp.einsum(
        "nhd,hde->nhe", queries, summary_b, preferred_element_type=jnp.float32
    ).reshape(row_count, feat_width)
    mean_val = jnp.mean(attended, axis=1, keepdims=True)
    centered = attended - mean_val
    var_val = jnp.mean(centered * centered, axis=1, keepdims=True)
    glob = centered * lax.rsqrt(var_val + norm_eps) * norm_gain[None, :]
    gate = jnp.dot(node_feats, w_gate, preferred_element_type=jnp.float32)
    base = node_feats.astype(jnp.float32) + glob
    total = base + jnp.concatenate(columns, axis=1).astype(jnp.float32) * gate
    return total.astype(jnp.bfloat16)


def solution(mesh):
    in_specs = (
        P(("blk", "grp"), None),
        P(),
        P(),
        P(),
        P(),
        P(),
        P(),
        P("blk", None, "grp", None, None, None),
        P("blk", None, "grp", None),
        P("blk", None, "grp"),
    )
    out_specs = P(("blk", "grp"), None)
    return jax.shard_map(local, mesh=mesh, in_specs=in_specs, out_specs=out_specs, check_vma=False)
```

time: 634 us -> 133 us (0.21); the launches traced: 626 us -> 132 us
  loops' own time: 212 us -> 0 us
  other arithmetic: 206 us -> 4.55 us
  blocking collectives: 54.8 us -> 0 us
  starting transfers between devices: 12 us -> 43.4 us
  between operations: 29.6 us -> 0.56 us
  local copies, waits for them, and re-layouts: 43.4 us -> 18.7 us
  matrix products: 36.7 us -> 17.5 us
  waiting for transfers between devices: 31.4 us -> 44.5 us
    another operation x2 -> x0, loops' own time: 212 us -> none  [one_hop(): lax.fori_loop(0, blocks - 1, turn, (feats, empty))]
    dynamic_update_slice x128 -> x0, other arithmetic: 199 us -> none  [accumulate(): lax.dynamic_update_index_in_dim(partial_value, current + product[slot], t...]
    ppermute x14 -> x35, waiting for transfers between devices: 0.04 us -> 44.5 us  [swap(): return lax.ppermute(value, axis, [(i, i ^ mask) for i in range(size)])]
    psum x1 -> x0, blocking collectives: 42.5 us -> none  [local(): summary = lax.psum(local_flat, ('blk', 'grp'))]
    reduce_scatter x2 -> x0, waiting for transfers between devices: 31.4 us -> none  [the longest x1 31.4 us: local(): lax.psum_scatter(flat, 'grp', scatter_dimension=0, tiled=True)]
    ppermute x14 -> x35, starting transfers between devices: 12 us -> 43.4 us  [swap(): return lax.ppermute(value, axis, [(i, i ^ mask) for i in range(size)])]
    gather x16 -> x0, local copies, waits for them, and re-layouts: 25.3 us -> none  [accumulate(): chosen = jnp.take(stacked, cols_here, axis=0)]
    dot_general x17 -> x4, matrix products: 30.7 us -> 10.4 us  [one_hop(): jnp.dot(adjacency, gathered.reshape(blocks * row_count, -1), preferred_el...]
  transfers between devices with their start and end apart: 16 -> 35, of which waited for: 1 -> 16; matrix products, arithmetic and copies ran while one was open for 40% -> 20% of each run, Pallas kernels for 0% -> 2%
where the time goes in v1:
time: 133 us; the launch traced here: 132 us
  waiting for transfers between devices  44.5 us (33%)
  starting transfers between devices  43.4 us (33%)
  local copies, waits for them, and re-layouts  18.7 us (14%)
  matrix products  17.5 us (13%)
  other arithmetic  4.55 us (3%)
  Pallas kernels  3.06 us (2%)
    ppermute x35, waiting for transfers between devices, swap(): return lax.ppermute(value, axis, [(i, i ^ mask) for i in range(size)])  44.5 us
    ppermute x35, starting transfers between devices, swap(): return lax.ppermute(value, axis, [(i, i ^ mask) for i in range(size)])  43.4 us
    unnamed x32, local copies, waits for them, and re-layouts  10.5 us
    dot_general x4, matrix products, one_hop(): jnp.dot(adjacency, gathered.reshape(blocks * row_count, -1), preferred_el...  10.4 us
    pallas_call x1, Pallas kernels, prepare(): pl.pallas_call(kernel, out_shape=(jax.ShapeDtypeStruct((rows, blocks * co...  3.06 us
    convert_element_type x2, other arithmetic, one_hop(): return (total * scale).astype(jnp.bfloat16)  2.7 us
  transfers between devices with their start and end apart: 35, of which 16 were waited for; matrix products, arithmetic and copies ran while one was open for 20% of the time, Pallas kernels for 2%

profile of v1, /device:TPU:0, one launch (start us, length us, event | category | flops | bytes accessed | tf_op | source)
XLA Modules:
  0.0 132.2 jit_solution(12177364879580072847)
XLA Ops:
  5.3 2.6 %collective-permute-start.21 = (bf16[256,256]{1,0:T(8,128)(2,1)S(1)}, bf16[256,256]{1,0:T(8,128)(2,1)S(1)}, u32[]{:S(2)}, u32[]{:S(2)}) collective-permute-start(bf16[256,256]{1,0:T(8,128)(2,1)S(1)} %get-tuple-element.24), channel_id=1, source_target_pairs={{0,8},{4,12},{8,0},{12,4},{16,24},{20,28},{24,16},{28,20},{1,9},{5... | collective-permute-start | bytes 393224 | tf_op jit(solution)/shard_map/ppermute | solution.py:18
  7.9 1.5 %collective-permute-start.22 = (bf16[256,256]{1,0:T(8,128)(2,1)S(1)}, bf16[256,256]{1,0:T(8,128)(2,1)S(1)}, u32[]{:S(2)}, u32[]{:S(2)}) collective-permute-start(bf16[256,256]{1,0:T(8,128)(2,1)S(1)} %get-tuple-element.24), channel_id=1, source_target_pairs={{0,16},{4,20},{8,24},{12,28},{16,0},{20,4},{24,8},{28,12},{1,17},{... | collective-permute-start | bytes 393224 | tf_op jit(solution)/shard_map/ppermute | solution.py:18
  9.4 2.0 %collective-permute-start.1 = (f32[256,128]{1,0:T(8,128)S(1)}, f32[256,128]{1,0:T(8,128)S(1)}, u32[]{:S(2)}, u32[]{:S(2)}) collective-permute-start(f32[256,128]{1,0:T(8,128)S(1)} %add.127), channel_id=1, source_target_pairs={{0,8},{4,12},{8,0},{12,4},{16,24},{20,28},{24,16},{28,20},{1,9},{5... | collective-permute-start | bytes 393224 | tf_op jit(solution)/shard_map/ppermute | solution.py:18
  12.2 3.7 %collective-permute-done.22 = bf16[256,256]{1,0:T(8,128)(2,1)S(1)} collective-permute-done((bf16[256,256]{1,0:T(8,128)(2,1)S(1)}, bf16[256,256]{1,0:T(8,128)(2,1)S(1)}, u32[]{:S(2)}, u32[]{:S(2)}) %collective-permute-start.22) | collective-permute-done | bytes 131104 | tf_op jit(solution)/shard_map/ppermute | solution.py:18
  16.9 2.2 %copy-done.1 = s32[1,8,1,8,128,128]{5,4,3,2,1,0:T(8,128)S(1)} copy-done((s32[1,8,1,8,128,128]{5,4,3,2,1,0:T(8,128)S(1)}, s32[1,8,1,8,128,128]{5,4,3,2,1,0:T(8,128)}, u32[]{:S(2)}) %copy-start.1) | copy-done | bytes 4194328
  19.0 3.1 %prepare.1 = (bf16[1024,2048]{1,0:T(8,128)(2,1)S(1)}, f32[8,1024]{1,0:T(8,128)S(1)}) custom-call(s32[1]{0:T(128)} %bitcast.5.me_ref, s32[8,8]{1,0:T(8,128)S(1)} %bitcast.136, s32[8]{0:T(128)S(1)} %bitcast.137, s32[8,8,128,128]{3,2,1,0:T(8,128)S(1)} %bitcast.135), custom_call_target="tpu_custom_call" | custom-call | flops 2097152 | bytes 8388608 | tf_op jit(solution)/shard_map/prepare/pallas_call | solution.py:53
  22.1 2.0 %copy-done.4 = bf16[1024,2048]{1,0:T(8,128)(2,1)} copy-done((bf16[1024,2048]{1,0:T(8,128)(2,1)}, bf16[1024,2048]{1,0:T(8,128)(2,1)S(1)}, u32[]{:S(2)}) %copy-start.4) | copy-done | bytes 4194328
  24.1 1.6 %collective-permute-start.12 = (f32[1024]{0:T(1024)S(1)}, f32[1024]{0:T(1024)S(1)}, u32[]{:S(2)}, u32[]{:S(2)}) collective-permute-start(f32[1024]{0:T(1024)S(1)} %bitcast.155), channel_id=1, source_target_pairs={{0,1},{1,0},{2,3},{3,2},{4,5},{5,4},{6,7},{7,6},{8,9},{9,8},{10,11... | collective-permute-start | bytes 12296 | tf_op jit(solution)/shard_map/ppermute | solution.py:18
  25.6 2.0 %collective-permute-done.12 = f32[1024]{0:T(1024)S(1)} collective-permute-done((f32[1024]{0:T(1024)S(1)}, f32[1024]{0:T(1024)S(1)}, u32[]{:S(2)}, u32[]{:S(2)}) %collective-permute-start.12) | collective-permute-done | bytes 4128 | tf_op jit(solution)/shard_map/ppermute | solution.py:18
  27.7 2.4 %collective-permute-start.13 = (f32[1024]{0:T(1024)S(1)}, f32[1024]{0:T(1024)S(1)}, u32[]{:S(2)}, u32[]{:S(2)}) collective-permute-start(f32[1024]{0:T(1024)S(1)} %add.144), channel_id=1, source_target_pairs={{0,2},{1,3},{2,0},{3,1},{4,6},{5,7},{6,4},{7,5},{8,10},{9,11},{10,... | collective-permute-start | bytes 12296 | tf_op jit(solution)/shard_map/ppermute | solution.py:18
  31.9 1.7 %collective-permute-start.7 = (bf16[256,256]{1,0:T(8,128)(2,1)S(1)}, bf16[256,256]{1,0:T(8,128)(2,1)S(1)}, u32[]{:S(2)}, u32[]{:S(2)}) collective-permute-start(bf16[256,256]{1,0:T(8,128)(2,1)S(1)} %get-tuple-element.23), channel_id=1, source_target_pairs={{0,24},{4,28},{8,16},{12,20},{16,8},{20,12},{24,0},{28,4},{1,25},{... | collective-permute-start | bytes 393224 | tf_op jit(solution)/shard_map/ppermute | solution.py:18
  36.4 4.7 %collective-permute-done.2 = f32[256,128]{1,0:T(8,128)S(1)} collective-permute-done((f32[256,128]{1,0:T(8,128)S(1)}, f32[256,128]{1,0:T(8,128)S(1)}, u32[]{:S(2)}, u32[]{:S(2)}) %collective-permute-start.2) | collective-permute-done | bytes 131104 | tf_op jit(solution)/shard_map/ppermute | solution.py:18
  41.2 1.8 %collective-permute-start.3 = (f32[256,128]{1,0:T(8,128)S(1)}, f32[256,128]{1,0:T(8,128)S(1)}, u32[]{:S(2)}, u32[]{:S(2)}) collective-permute-start(f32[256,128]{1,0:T(8,128)S(1)} %add.129), channel_id=1, source_target_pairs={{0,1},{1,0},{2,3},{3,2},{4,5},{5,4},{6,7},{7,6},{8,9},{9,8},{10,11... | collective-permute-start | bytes 393224 | tf_op jit(solution)/shard_map/ppermute | solution.py:18
  43.1 3.2 %collective-permute-done.3 = f32[256,128]{1,0:T(8,128)S(1)} collective-permute-done((f32[256,128]{1,0:T(8,128)S(1)}, f32[256,128]{1,0:T(8,128)S(1)}, u32[]{:S(2)}, u32[]{:S(2)}) %collective-permute-start.3) | collective-permute-done | bytes 131104 | tf_op jit(solution)/shard_map/ppermute | solution.py:18
  48.3 4.6 %collective-permute-start.25 = (bf16[256,256]{1,0:T(8,128)(2,1)S(1)}, bf16[256,256]{1,0:T(8,128)(2,1)S(1)}, u32[]{:S(2)}, u32[]{:S(2)}) collective-permute-start(bf16[256,256]{1,0:T(8,128)(2,1)S(1)} %get-tuple-element.18), channel_id=1, source_target_pairs={{0,3},{1,2},{2,1},{3,0},{4,7},{5,6},{6,5},{7,4},{8,11},{9,10},{10,... | collective-permute-start | bytes 393224 | tf_op jit(solution)/shard_map/ppermute | solution.py:18
  53.6 2.3 %fusion.41 = f32[4,256,256]{2,1,0:T(8,128)} fusion(bf16[4,256,2048]{2,1,0:T(8,128)(2,1)S(1)} %bitcast.141, bf16[2048,256,1]{1,0,2:T(8,128)(2,1)S(1)} %bitcast.150), kind=kOutput, calls=%fused_computation.83 | convolution fusion | flops 1073741824 | bytes 6291456 | tf_op jit(solution)/shard_map/dot_general | solution.py:124
  57.1 2.3 %collective-permute-start.10 = (bf16[256,256]{1,0:T(8,128)(2,1)S(1)}, bf16[256,256]{1,0:T(8,128)(2,1)S(1)}, u32[]{:S(2)}, u32[]{:S(2)}) collective-permute-start(bf16[256,256]{1,0:T(8,128)(2,1)S(1)} %get-tuple-element.14), channel_id=1, source_target_pairs={{0,2},{1,3},{2,0},{3,1},{4,6},{5,7},{6,4},{7,5},{8,10},{9,11},{10,... | collective-permute-start | bytes 393224 | tf_op jit(solution)/shard_map/ppermute | solution.py:18
  59.4 1.9 %collective-permute-done.4 = f32[256,128]{1,0:T(8,128)S(1)} collective-permute-done((f32[256,128]{1,0:T(8,128)S(1)}, f32[256,128]{1,0:T(8,128)S(1)}, u32[]{:S(2)}, u32[]{:S(2)}) %collective-permute-start.4) | collective-permute-done | bytes 131104 | tf_op jit(solution)/shard_map/ppermute | solution.py:18
  61.4 2.0 %collective-permute-start.9 = (bf16[256,256]{1,0:T(8,128)(2,1)S(1)}, bf16[256,256]{1,0:T(8,128)(2,1)}, u32[]{:S(2)}, u32[]{:S(2)}) collective-permute-start(bf16[256,256]{1,0:T(8,128)(2,1)S(1)} %get-tuple-element.12), channel_id=1, source_target_pairs={{0,3},{1,2},{2,1},{3,0},{4,7},{5,6},{6,5},{7,4},{8,11},{9,10},{10,... | collective-permute-start | bytes 393224 | tf_op jit(solution)/shard_map/ppermute | solution.py:18
  63.6 7.6 %collective-permute-done.26 = bf16[256,256]{1,0:T(8,128)(2,1)} collective-permute-done((bf16[256,256]{1,0:T(8,128)(2,1)S(1)}, bf16[256,256]{1,0:T(8,128)(2,1)}, u32[]{:S(2)}, u32[]{:S(2)}) %collective-permute-start.26) | collective-permute-done | bytes 131104 | tf_op jit(solution)/shard_map/ppermute | solution.py:18
  71.2 2.7 %collective-permute-done.10 = bf16[256,256]{1,0:T(8,128)(2,1)S(1)} collective-permute-done((bf16[256,256]{1,0:T(8,128)(2,1)S(1)}, bf16[256,256]{1,0:T(8,128)(2,1)S(1)}, u32[]{:S(2)}, u32[]{:S(2)}) %collective-permute-start.10) | collective-permute-done | bytes 131104 | tf_op jit(solution)/shard_map/ppermute | solution.py:18
  75.9 1.5 %collective-permute-start.28 = (bf16[256,256]{1,0:T(8,128)(2,1)S(1)}, bf16[256,256]{1,0:T(8,128)(2,1)S(1)}, u32[]{:S(2)}, u32[]{:S(2)}) collective-permute-start(bf16[256,256]{1,0:T(8,128)(2,1)S(1)} %get-tuple-element.22), channel_id=1, source_target_pairs={{0,8},{4,12},{8,0},{12,4},{16,24},{20,28},{24,16},{28,20},{1,9},{5... | collective-permute-start | bytes 393224 | tf_op jit(solution)/shard_map/ppermute | solution.py:18
  85.1 1.5 %collective-permute-start.14 = (bf16[256,256]{1,0:T(8,128)(2,1)S(1)}, bf16[256,256]{1,0:T(8,128)(2,1)S(1)}, u32[]{:S(2)}, u32[]{:S(2)}) collective-permute-start(bf16[256,256]{1,0:T(8,128)(2,1)S(1)} %get-tuple-element.21), channel_id=1, source_target_pairs={{0,8},{4,12},{8,0},{12,4},{16,24},{20,28},{24,16},{28,20},{1,9},{5... | collective-permute-start | bytes 393224 | tf_op jit(solution)/shard_map/ppermute | solution.py:18
  88.7 2.8 %collective-permute-done.14 = bf16[256,256]{1,0:T(8,128)(2,1)S(1)} collective-permute-done((bf16[256,256]{1,0:T(8,128)(2,1)S(1)}, bf16[256,256]{1,0:T(8,128)(2,1)S(1)}, u32[]{:S(2)}, u32[]{:S(2)}) %collective-permute-start.14) | collective-permute-done | bytes 131104 | tf_op jit(solution)/shard_map/ppermute | solution.py:18
  91.5 3.6 %collective-permute-done.15 = bf16[256,256]{1,0:T(8,128)(2,1)S(1)} collective-permute-done((bf16[256,256]{1,0:T(8,128)(2,1)S(1)}, bf16[256,256]{1,0:T(8,128)(2,1)S(1)}, u32[]{:S(2)}, u32[]{:S(2)}) %collective-permute-start.15) | collective-permute-done | bytes 131104 | tf_op jit(solution)/shard_map/ppermute | solution.py:18
  97.3 3.5 %fusion.44 = f32[4,256,256]{1,2,0:T(8,128)S(1)} fusion(bf16[4,256,2048]{2,1,0:T(8,128)(2,1)} %bitcast.138, bf16[2048,256,1]{0,1,2:T(8,128)(2,1)S(1)} %reshape.82), kind=kOutput, calls=%fused_computation.86 | convolution fusion | flops 1073741824 | bytes 6291456 | tf_op jit(solution)/shard_map/dot_general | solution.py:124
  101.7 1.6 %collective-permute-start.32 = (bf16[256,256]{1,0:T(8,128)(2,1)}, bf16[256,256]{1,0:T(8,128)(2,1)S(1)}, u32[]{:S(2)}, u32[]{:S(2)}) collective-permute-start(bf16[256,256]{1,0:T(8,128)(2,1)} %bitcast.109), channel_id=1, source_target_pairs={{0,3},{1,2},{2,1},{3,0},{4,7},{5,6},{6,5},{7,4},{8,11},{9,10},{10,... | collective-permute-start | bytes 393224 | tf_op jit(solution)/shard_map/ppermute | solution.py:18
  110.7 3.5 %fusion.42 = f32[4,256,256]{1,2,0:T(8,128)S(1)} fusion(bf16[4,256,2048]{2,1,0:T(8,128)(2,1)} %bitcast.139, bf16[2048,256,1]{0,1,2:T(8,128)(2,1)S(1)} %reshape.80), kind=kOutput, calls=%fused_computation.84 | convolution fusion | flops 1073741824 | bytes 6291456 | tf_op jit(solution)/shard_map/dot_general | solution.py:124
  115.0 1.6 %collective-permute-start.18 = (bf16[256,256]{1,0:T(8,128)(2,1)}, bf16[256,256]{1,0:T(8,128)(2,1)}, u32[]{:S(2)}, u32[]{:S(2)}) collective-permute-start(bf16[256,256]{1,0:T(8,128)(2,1)} %bitcast.112), channel_id=1, source_target_pairs={{0,3},{1,2},{2,1},{3,0},{4,7},{5,6},{6,5},{7,4},{8,11},{9,10},{10,... | collective-permute-start | bytes 393224 | tf_op jit(solution)/shard_map/ppermute | solution.py:18
  118.5 2.4 %collective-permute-start.20 = (bf16[256,256]{1,0:T(8,128)(2,1)}, bf16[256,256]{1,0:T(8,128)(2,1)}, u32[]{:S(2)}, u32[]{:S(2)}) collective-permute-start(bf16[256,256]{1,0:T(8,128)(2,1)} %bitcast.110), channel_id=1, source_target_pairs={{0,1},{1,0},{2,3},{3,2},{4,5},{5,4},{6,7},{7,6},{8,9},{9,8},{10,11... | collective-permute-start | bytes 393224 | tf_op jit(solution)/shard_map/ppermute | solution.py:18
  123.6 5.2 %collective-permute-done.19 = bf16[256,256]{1,0:T(8,128)(2,1)} collective-permute-done((bf16[256,256]{1,0:T(8,128)(2,1)}, bf16[256,256]{1,0:T(8,128)(2,1)}, u32[]{:S(2)}, u32[]{:S(2)}) %collective-permute-start.19) | collective-permute-done | bytes 131104 | tf_op jit(solution)/shard_map/ppermute | solution.py:18
  130.1 2.1 %fusion.7 = bf16[256,512]{1,0:T(8,128)(2,1)} fusion(bf16[256,512]{1,0:T(8,128)(2,1)S(1)} %copy-done.7, bf16[512,512]{1,0:T(8,128)(2,1)} %param.12, f32[256,512]{1,0:T(8,128)S(1)} %copy-done.9, bf16[256,256]{1,0:T(8,128)(2,1)S(1)} %get-tuple-element.26, bf16[256,256]{1,0:T(8,128)(2,1)S(1)} %get-tuple-element.25, f32[512]{0:T(512)S(1)} %copy-done.12, ...), kind=kOutput, calls=%fused_computation.10 | convolution fusion | flops 135790592 | bytes 1839104 | tf_op jit(solution)/shard_map/dot_general | solution.py:169
  (125 shorter events, 44.8 us)
Async XLA Ops:
  5.3 6.9 %collective-permute-start.21 = (bf16[256,256]{1,0:T(8,128)(2,1)S(1)}, bf16[256,256]{1,0:T(8,128)(2,1)S(1)}, u32[]{:S(2)}, u32[]{:S(2)}) collective-permute-start(bf16[256,256]{1,0:T(8,128)(2,1)S(1)} %get-tuple-element.24), channel_id=1, source_target_pairs={{0,8},{4,12},{8,0},{12,4},{16,24},{20,28},{24,16},{28,20},{1,9},{5... | collective-permute-start | bytes 393224 | tf_op jit(solution)/shard_map/ppermute | solution.py:18
  7.9 8.0 %collective-permute-start.22 = (bf16[256,256]{1,0:T(8,128)(2,1)S(1)}, bf16[256,256]{1,0:T(8,128)(2,1)S(1)}, u32[]{:S(2)}, u32[]{:S(2)}) collective-permute-start(bf16[256,256]{1,0:T(8,128)(2,1)S(1)} %get-tuple-element.24), channel_id=1, source_target_pairs={{0,16},{4,20},{8,24},{12,28},{16,0},{20,4},{24,8},{28,12},{1,17},{... | collective-permute-start | bytes 393224 | tf_op jit(solution)/shard_map/ppermute | solution.py:18
  9.4 7.3 %collective-permute-start.23 = (bf16[256,256]{1,0:T(8,128)(2,1)S(1)}, bf16[256,256]{1,0:T(8,128)(2,1)S(1)}, u32[]{:S(2)}, u32[]{:S(2)}) collective-permute-start(bf16[256,256]{1,0:T(8,128)(2,1)S(1)} %get-tuple-element.24), channel_id=1, source_target_pairs={{0,24},{4,28},{8,16},{12,20},{16,8},{20,12},{24,0},{28,4},{1,25},{... | collective-permute-start | bytes 393224 | tf_op jit(solution)/shard_map/ppermute | solution.py:18
  9.4 22.5 %collective-permute-start.1 = (f32[256,128]{1,0:T(8,128)S(1)}, f32[256,128]{1,0:T(8,128)S(1)}, u32[]{:S(2)}, u32[]{:S(2)}) collective-permute-start(f32[256,128]{1,0:T(8,128)S(1)} %add.127), channel_id=1, source_target_pairs={{0,8},{4,12},{8,0},{12,4},{16,24},{20,28},{24,16},{28,20},{1,9},{5... | collective-permute-start | bytes 393224 | tf_op jit(solution)/shard_map/ppermute | solution.py:18
  16.7 30.0 %collective-permute-start.24 = (bf16[1024,256]{1,0:T(8,128)(2,1)S(1)}, bf16[1024,256]{1,0:T(8,128)(2,1)S(1)}, u32[]{:S(2)}, u32[]{:S(2)}) collective-permute-start(bf16[1024,256]{1,0:T(8,128)(2,1)S(1)} %pad_maximum_fusion.6), channel_id=1, source_target_pairs={{0,4},{4,0},{8,12},{12,8},{16,20},{20,16},{24,28},{28,24},{1,5},{5... | collective-permute-start | bytes 1572872 | tf_op jit(solution)/shard_map/ppermute | solution.py:18
  27.7 5.9 %collective-permute-start.13 = (f32[1024]{0:T(1024)S(1)}, f32[1024]{0:T(1024)S(1)}, u32[]{:S(2)}, u32[]{:S(2)}) collective-permute-start(f32[1024]{0:T(1024)S(1)} %add.144), channel_id=1, source_target_pairs={{0,2},{1,3},{2,0},{3,1},{4,6},{5,7},{6,4},{7,5},{8,10},{9,11},{10,... | collective-permute-start | bytes 12296 | tf_op jit(solution)/shard_map/ppermute | solution.py:18
  30.1 12.9 %collective-permute-start.5 = (bf16[256,256]{1,0:T(8,128)(2,1)S(1)}, bf16[256,256]{1,0:T(8,128)(2,1)S(1)}, u32[]{:S(2)}, u32[]{:S(2)}) collective-permute-start(bf16[256,256]{1,0:T(8,128)(2,1)S(1)} %get-tuple-element.23), channel_id=1, source_target_pairs={{0,8},{4,12},{8,0},{12,4},{16,24},{20,28},{24,16},{28,20},{1,9},{5... | collective-permute-start | bytes 393224 | tf_op jit(solution)/shard_map/ppermute | solution.py:18
  31.4 11.5 %collective-permute-start.6 = (bf16[256,256]{1,0:T(8,128)(2,1)S(1)}, bf16[256,256]{1,0:T(8,128)(2,1)S(1)}, u32[]{:S(2)}, u32[]{:S(2)}) collective-permute-start(bf16[256,256]{1,0:T(8,128)(2,1)S(1)} %get-tuple-element.23), channel_id=1, source_target_pairs={{0,16},{4,20},{8,24},{12,28},{16,0},{20,4},{24,8},{28,12},{1,17},{... | collective-permute-start | bytes 393224 | tf_op jit(solution)/shard_map/ppermute | solution.py:18
  31.9 11.1 %collective-permute-start.7 = (bf16[256,256]{1,0:T(8,128)(2,1)S(1)}, bf16[256,256]{1,0:T(8,128)(2,1)S(1)}, u32[]{:S(2)}, u32[]{:S(2)}) collective-permute-start(bf16[256,256]{1,0:T(8,128)(2,1)S(1)} %get-tuple-element.23), channel_id=1, source_target_pairs={{0,24},{4,28},{8,16},{12,20},{16,8},{20,12},{24,0},{28,4},{1,25},{... | collective-permute-start | bytes 393224 | tf_op jit(solution)/shard_map/ppermute | solution.py:18
  33.6 7.5 %collective-permute-start.2 = (f32[256,128]{1,0:T(8,128)S(1)}, f32[256,128]{1,0:T(8,128)S(1)}, u32[]{:S(2)}, u32[]{:S(2)}) collective-permute-start(f32[256,128]{1,0:T(8,128)S(1)} %add.128), channel_id=1, source_target_pairs={{0,16},{4,20},{8,24},{12,28},{16,0},{20,4},{24,8},{28,12},{1,17},{... | collective-permute-start | bytes 393224 | tf_op jit(solution)/shard_map/ppermute | solution.py:18
  41.2 5.2 %collective-permute-start.3 = (f32[256,128]{1,0:T(8,128)S(1)}, f32[256,128]{1,0:T(8,128)S(1)}, u32[]{:S(2)}, u32[]{:S(2)}) collective-permute-start(f32[256,128]{1,0:T(8,128)S(1)} %add.129), channel_id=1, source_target_pairs={{0,1},{1,0},{2,3},{3,2},{4,5},{5,4},{6,7},{7,6},{8,9},{9,8},{10,11... | collective-permute-start | bytes 393224 | tf_op jit(solution)/shard_map/ppermute | solution.py:18
  43.0 10.4 %collective-permute-start.8 = (bf16[1024,256]{1,0:T(8,128)(2,1)S(1)}, bf16[1024,256]{1,0:T(8,128)(2,1)S(1)}, u32[]{:S(2)}, u32[]{:S(2)}) collective-permute-start(bf16[1024,256]{1,0:T(8,128)(2,1)S(1)} %pad_maximum_fusion.4), channel_id=1, source_target_pairs={{0,4},{4,0},{8,12},{12,8},{16,20},{20,16},{24,28},{28,24},{1,5},{5... | collective-permute-start | bytes 1572872 | tf_op jit(solution)/shard_map/ppermute | solution.py:18
  46.3 14.9 %collective-permute-start.4 = (f32[256,128]{1,0:T(8,128)S(1)}, f32[256,128]{1,0:T(8,128)S(1)}, u32[]{:S(2)}, u32[]{:S(2)}) collective-permute-start(f32[256,128]{1,0:T(8,128)S(1)} %add.130), channel_id=1, source_target_pairs={{0,2},{1,3},{2,0},{3,1},{4,6},{5,7},{6,4},{7,5},{8,10},{9,11},{10,... | collective-permute-start | bytes 393224 | tf_op jit(solution)/shard_map/ppermute | solution.py:18
  48.3 13.2 %collective-permute-start.25 = (bf16[256,256]{1,0:T(8,128)(2,1)S(1)}, bf16[256,256]{1,0:T(8,128)(2,1)S(1)}, u32[]{:S(2)}, u32[]{:S(2)}) collective-permute-start(bf16[256,256]{1,0:T(8,128)(2,1)S(1)} %get-tuple-element.18), channel_id=1, source_target_pairs={{0,3},{1,2},{2,1},{3,0},{4,7},{5,6},{6,5},{7,4},{8,11},{9,10},{10,... | collective-permute-start | bytes 393224 | tf_op jit(solution)/shard_map/ppermute | solution.py:18
  52.8 18.4 %collective-permute-start.26 = (bf16[256,256]{1,0:T(8,128)(2,1)S(1)}, bf16[256,256]{1,0:T(8,128)(2,1)}, u32[]{:S(2)}, u32[]{:S(2)}) collective-permute-start(bf16[256,256]{1,0:T(8,128)(2,1)S(1)} %get-tuple-element.20), channel_id=1, source_target_pairs={{0,2},{1,3},{2,0},{3,1},{4,6},{5,7},{6,4},{7,5},{8,10},{9,11},{10,... | collective-permute-start | bytes 393224 | tf_op jit(solution)/shard_map/ppermute | solution.py:18
  52.8 18.4 %collective-permute-start.27 = (bf16[256,256]{1,0:T(8,128)(2,1)S(1)}, bf16[256,256]{1,0:T(8,128)(2,1)}, u32[]{:S(2)}, u32[]{:S(2)}) collective-permute-start(bf16[256,256]{1,0:T(8,128)(2,1)S(1)} %get-tuple-element.19), channel_id=1, source_target_pairs={{0,1},{1,0},{2,3},{3,2},{4,5},{5,4},{6,7},{7,6},{8,9},{9,8},{10,11... | collective-permute-start | bytes 393224 | tf_op jit(solution)/shard_map/ppermute | solution.py:18
  57.1 16.8 %collective-permute-start.10 = (bf16[256,256]{1,0:T(8,128)(2,1)S(1)}, bf16[256,256]{1,0:T(8,128)(2,1)S(1)}, u32[]{:S(2)}, u32[]{:S(2)}) collective-permute-start(bf16[256,256]{1,0:T(8,128)(2,1)S(1)} %get-tuple-element.14), channel_id=1, source_target_pairs={{0,2},{1,3},{2,0},{3,1},{4,6},{5,7},{6,4},{7,5},{8,10},{9,11},{10,... | collective-permute-start | bytes 393224 | tf_op jit(solution)/shard_map/ppermute | solution.py:18
  61.3 12.6 %collective-permute-start.11 = (bf16[256,256]{1,0:T(8,128)(2,1)S(1)}, bf16[256,256]{1,0:T(8,128)(2,1)}, u32[]{:S(2)}, u32[]{:S(2)}) collective-permute-start(bf16[256,256]{1,0:T(8,128)(2,1)S(1)} %get-tuple-element.13), channel_id=1, source_target_pairs={{0,1},{1,0},{2,3},{3,2},{4,5},{5,4},{6,7},{7,6},{8,9},{9,8},{10,11... | collective-permute-start | bytes 393224 | tf_op jit(solution)/shard_map/ppermute | solution.py:18
  61.4 13.1 %collective-permute-start.9 = (bf16[256,256]{1,0:T(8,128)(2,1)S(1)}, bf16[256,256]{1,0:T(8,128)(2,1)}, u32[]{:S(2)}, u32[]{:S(2)}) collective-permute-start(bf16[256,256]{1,0:T(8,128)(2,1)S(1)} %get-tuple-element.12), channel_id=1, source_target_pairs={{0,3},{1,2},{2,1},{3,0},{4,7},{5,6},{6,5},{7,4},{8,11},{9,10},{10,... | collective-permute-start | bytes 393224 | tf_op jit(solution)/shard_map/ppermute | solution.py:18
  75.9 5.2 %collective-permute-start.28 = (bf16[256,256]{1,0:T(8,128)(2,1)S(1)}, bf16[256,256]{1,0:T(8,128)(2,1)S(1)}, u32[]{:S(2)}, u32[]{:S(2)}) collective-permute-start(bf16[256,256]{1,0:T(8,128)(2,1)S(1)} %get-tuple-element.22), channel_id=1, source_target_pairs={{0,8},{4,12},{8,0},{12,4},{16,24},{20,28},{24,16},{28,20},{1,9},{5... | collective-permute-start | bytes 393224 | tf_op jit(solution)/shard_map/ppermute | solution.py:18
  78.0 5.9 %collective-permute-start.30 = (bf16[256,256]{1,0:T(8,128)(2,1)S(1)}, bf16[256,256]{1,0:T(8,128)(2,1)S(1)}, u32[]{:S(2)}, u32[]{:S(2)}) collective-permute-start(bf16[256,256]{1,0:T(8,128)(2,1)S(1)} %get-tuple-element.22), channel_id=1, source_target_pairs={{0,24},{4,28},{8,16},{12,20},{16,8},{20,12},{24,0},{28,4},{1,25},{... | collective-permute-start | bytes 393224 | tf_op jit(solution)/shard_map/ppermute | solution.py:18
  83.9 11.3 %collective-permute-start.31 = (bf16[1024,256]{1,0:T(8,128)(2,1)S(1)}, bf16[1024,256]{1,0:T(8,128)(2,1)S(1)}, u32[]{:S(2)}, u32[]{:S(2)}) collective-permute-start(bf16[1024,256]{1,0:T(8,128)(2,1)S(1)} %pad_maximum_fusion.7), channel_id=1, source_target_pairs={{0,4},{4,0},{8,12},{12,8},{16,20},{20,16},{24,28},{28,24},{1,5},{5... | collective-permute-start | bytes 1572872 | tf_op jit(solution)/shard_map/ppermute | solution.py:18
  85.1 6.4 %collective-permute-start.14 = (bf16[256,256]{1,0:T(8,128)(2,1)S(1)}, bf16[256,256]{1,0:T(8,128)(2,1)S(1)}, u32[]{:S(2)}, u32[]{:S(2)}) collective-permute-start(bf16[256,256]{1,0:T(8,128)(2,1)S(1)} %get-tuple-element.21), channel_id=1, source_target_pairs={{0,8},{4,12},{8,0},{12,4},{16,24},{20,28},{24,16},{28,20},{1,9},{5... | collective-permute-start | bytes 393224 | tf_op jit(solution)/shard_map/ppermute | solution.py:18
  86.7 8.4 %collective-permute-start.15 = (bf16[256,256]{1,0:T(8,128)(2,1)S(1)}, bf16[256,256]{1,0:T(8,128)(2,1)S(1)}, u32[]{:S(2)}, u32[]{:S(2)}) collective-permute-start(bf16[256,256]{1,0:T(8,128)(2,1)S(1)} %get-tuple-element.21), channel_id=1, source_target_pairs={{0,16},{4,20},{8,24},{12,28},{16,0},{20,4},{24,8},{28,12},{1,17},{... | collective-permute-start | bytes 393224 | tf_op jit(solution)/shard_map/ppermute | solution.py:18
  87.2 7.9 %collective-permute-start.16 = (bf16[256,256]{1,0:T(8,128)(2,1)S(1)}, bf16[256,256]{1,0:T(8,128)(2,1)S(1)}, u32[]{:S(2)}, u32[]{:S(2)}) collective-permute-start(bf16[256,256]{1,0:T(8,128)(2,1)S(1)} %get-tuple-element.21), channel_id=1, source_target_pairs={{0,24},{4,28},{8,16},{12,20},{16,8},{20,12},{24,0},{28,4},{1,25},{... | collective-permute-start | bytes 393224 | tf_op jit(solution)/shard_map/ppermute | solution.py:18
  95.1 12.5 %collective-permute-start.17 = (bf16[1024,256]{1,0:T(8,128)(2,1)S(1)}, bf16[1024,256]{1,0:T(8,128)(2,1)}, u32[]{:S(2)}, u32[]{:S(2)}) collective-permute-start(bf16[1024,256]{1,0:T(8,128)(2,1)S(1)} %pad_maximum_fusion.5), channel_id=1, source_target_pairs={{0,4},{4,0},{8,12},{12,8},{16,20},{20,16},{24,28},{28,24},{1,5},{5... | collective-permute-start | bytes 1572872 | tf_op jit(solution)/shard_map/ppermute | solution.py:18
  101.7 16.8 %collective-permute-start.32 = (bf16[256,256]{1,0:T(8,128)(2,1)}, bf16[256,256]{1,0:T(8,128)(2,1)S(1)}, u32[]{:S(2)}, u32[]{:S(2)}) collective-permute-start(bf16[256,256]{1,0:T(8,128)(2,1)} %bitcast.109), channel_id=1, source_target_pairs={{0,3},{1,2},{2,1},{3,0},{4,7},{5,6},{6,5},{7,4},{8,11},{9,10},{10,... | collective-permute-start | bytes 393224 | tf_op jit(solution)/shard_map/ppermute | solution.py:18
  104.1 18.1 %collective-permute-start.33 = (bf16[256,256]{1,0:T(8,128)(2,1)}, bf16[256,256]{1,0:T(8,128)(2,1)}, u32[]{:S(2)}, u32[]{:S(2)}) collective-permute-start(bf16[256,256]{1,0:T(8,128)(2,1)} %bitcast.108), channel_id=1, source_target_pairs={{0,2},{1,3},{2,0},{3,1},{4,6},{5,7},{6,4},{7,5},{8,10},{9,11},{10,... | collective-permute-start | bytes 393224 | tf_op jit(solution)/shard_map/ppermute | solution.py:18
  106.1 16.1 %collective-permute-start.34 = (bf16[256,256]{1,0:T(8,128)(2,1)}, bf16[256,256]{1,0:T(8,128)(2,1)}, u32[]{:S(2)}, u32[]{:S(2)}) collective-permute-start(bf16[256,256]{1,0:T(8,128)(2,1)} %bitcast.107), channel_id=1, source_target_pairs={{0,1},{1,0},{2,3},{3,2},{4,5},{5,4},{6,7},{7,6},{8,9},{9,8},{10,11... | collective-permute-start | bytes 393224 | tf_op jit(solution)/shard_map/ppermute | solution.py:18
  115.0 8.5 %collective-permute-start.18 = (bf16[256,256]{1,0:T(8,128)(2,1)}, bf16[256,256]{1,0:T(8,128)(2,1)}, u32[]{:S(2)}, u32[]{:S(2)}) collective-permute-start(bf16[256,256]{1,0:T(8,128)(2,1)} %bitcast.112), channel_id=1, source_target_pairs={{0,3},{1,2},{2,1},{3,0},{4,7},{5,6},{6,5},{7,4},{8,11},{9,10},{10,... | collective-permute-start | bytes 393224 | tf_op jit(solution)/shard_map/ppermute | solution.py:18
  117.4 11.4 %collective-permute-start.19 = (bf16[256,256]{1,0:T(8,128)(2,1)}, bf16[256,256]{1,0:T(8,128)(2,1)}, u32[]{:S(2)}, u32[]{:S(2)}) collective-permute-start(bf16[256,256]{1,0:T(8,128)(2,1)} %bitcast.111), channel_id=1, source_target_pairs={{0,2},{1,3},{2,0},{3,1},{4,6},{5,7},{6,4},{7,5},{8,10},{9,11},{10,... | collective-permute-start | bytes 393224 | tf_op jit(solution)/shard_map/ppermute | solution.py:18
  118.5 10.3 %collective-permute-start.20 = (bf16[256,256]{1,0:T(8,128)(2,1)}, bf16[256,256]{1,0:T(8,128)(2,1)}, u32[]{:S(2)}, u32[]{:S(2)}) collective-permute-start(bf16[256,256]{1,0:T(8,128)(2,1)} %bitcast.110), channel_id=1, source_target_pairs={{0,1},{1,0},{2,3},{3,2},{4,5},{5,4},{6,7},{7,6},{8,9},{9,8},{10,11... | collective-permute-start | bytes 393224 | tf_op jit(solution)/shard_map/ppermute | solution.py:18
  (16 other events, 128.2 us)
